TPU v7x, 256 devices: a whole 4x4x8 slice. The times are simulated.
256 devices in a mesh: group: 16 (over y, x), member: 16 (over z, core).
Axes of the slice: x: 4, y: 4, z: 8, core: 2. Of those that a mesh axis runs over, the one named last changes fastest.
Arguments:
- queries: bfloat16 [65536, 6144], P(('group', 'member')), may hold values from -64 to 64
- keys_values: bfloat16 [512, 128, 2048], P('group', 'member'), may hold values from -8 to 8
- local_lists: int32 [512, 5], P(('group', 'member')), may hold values from -1 to 31, as said below
- remote_lists: int32 [512, 3], P(('group', 'member')), may hold values from -1 to 15, as said below
- send_blocks: int32 [16, 16], P('group'), may hold values from 0 to 31
Outputs:
- attended: bfloat16 [65536, 6144], P(('group', 'member'))
Inputs may be any that keep to these rules, and one draw needn't show every extreme that they name: `local_lists`: row i lists distinct blocks of its slab, numbered 0 to 31 within the slab, then -1 in the remaining entries; the first entry is i mod 32, the row's own block. Some row lists 5 blocks. `remote_lists`: row i lists distinct slabs other than its own slab i // 32, then -1 in the remaining entries; a row may list none. Some row lists 3 slabs.
All inputs are finite; a program needn't handle non-finite values.
Results may differ from a plain program's by a relative error of at most 0.0038.
Values may be sent and summed in bfloat16 or wider, within the bound.
A program may use at most 128 MiB of HBM per device.

v0:
```python
import jax
import jax.numpy as jnp
from jax import lax
from jax.sharding import PartitionSpec as P

HEADS = 48
KV_HEADS = 8
HEAD_DIM = 128


def attend_rows(query_rows, listed, usable):
    block_rows = query_rows.shape[0]
    key_width = KV_HEADS * HEAD_DIM
    repeat = HEADS // KV_HEADS
    query_heads = query_rows.reshape(block_rows, KV_HEADS, repeat, HEAD_DIM)
    keys_all = listed[:, :, :key_width].reshape(
        listed.shape[0], listed.shape[1], KV_HEADS, HEAD_DIM
    )
    values_all = listed[:, :, key_width:].reshape(
        listed.shape[0], listed.shape[1], KV_HEADS, HEAD_DIM
    )
    halves = 2
    head_span = KV_HEADS // halves
    pieces = []
    for part_index in range(halves):
        start_head = part_index * head_span
        query_part = query_heads[:, start_head : start_head + head_span]
        keys_part = keys_all[:, :, start_head : start_head + head_span]
        values_part = values_all[:, :, start_head : start_head + head_span]
        scores = jnp.einsum(
            "qgrd,pkgd->qgrpk", query_part, keys_part, preferred_element_type=jnp.float32
        )
        scores = scores * HEAD_DIM ** (-0.5)
        scores = jnp.where(usable[:, None], scores, -jnp.inf)
        maxima = jnp.max(scores, axis=(3, 4), keepdims=True)
        weights = jnp.exp(scores - maxima)
        totals = jnp.sum(weights, axis=(3, 4))
        rounded = weights.astype(jnp.bfloat16)
        blended = jnp.einsum(
            "qgrpk,pkgd->qgrd", rounded, values_part, preferred_element_type=jnp.float32
        )
        pieces.append(blended / totals[..., None])
    joined = jnp.concatenate(pieces, axis=1)
    return joined.reshape(block_rows, HEADS * HEAD_DIM).astype(jnp.bfloat16)


def shards(queries, keys_values, local_lists, remote_lists, send_blocks):
    targets = send_blocks[0]
    query_count = local_lists.shape[0]
    block_rows = queries.shape[0] // query_count
    outputs = []
    outgoing = jnp.take(keys_values, targets, axis=0)
    arrived = lax.all_to_all(outgoing, "group", split_axis=0, concat_axis=0, tiled=True)
    group_pool = lax.all_gather(keys_values, "member", axis=1, tiled=True)
    cast_pool = lax.all_gather(arrived, "member", axis=1, tiled=True)
    for query_block in range(query_count):
        local_row = local_lists[query_block]
        remote_row = remote_lists[query_block]
        listed = jnp.concatenate(
            [
                jnp.take(group_pool, jnp.maximum(local_row, 0), axis=0),
                jnp.take(cast_pool, jnp.maximum(remote_row, 0), axis=0),
            ],
            axis=0,
        )
        usable = jnp.concatenate([local_row >= 0, remote_row >= 0])
        query_rows = queries[query_block * block_rows : (query_block + 1) * block_rows]
        outputs.append(attend_rows(query_rows, listed, usable))
    return jnp.concatenate(outputs, axis=0)


def solution(mesh):
    placed = (
        P(("group", "member"), None),
        P("group", "member", None),
        P(("group", "member"), None),
        P(("group", "member"), None),
        P("group", None),
    )
    return jax.shard_map(
        shards, mesh=mesh, in_specs=placed, out_specs=P(("group", "member"), None), check_vma=False
    )
```

profile of v0, /device:TPU:1, one launch (start us, length us, event | category | flops | bytes accessed | tf_op | source)
XLA Modules:
  0.0 306.8 jit_solution(815406715089342255)
XLA Ops:
  9.8 17.9 %all_to_all.5 = bf16[16,8,2048]{2,1,0:T(8,128)(2,1)} all-to-all(bf16[16,8,2048]{2,1,0:T(8,128)(2,1)S(1)} %broadcast_select_fusion.4), channel_id=1, replica_groups=mesh['group'=16,'member'=16] {'group'}, dimensions={0} | all-to-all | bytes 1048576 | tf_op jit(solution)/shard_map/all_to_all | solution.py:53
  34.0 50.6 %all-gather.5.cloned.1.call-done = bf16[16,128,2048]{2,1,0:T(8,128)(2,1)} async-done(((bf16[16,8,2048]{2,1,0:T(8,128)(2,1)}), bf16[16,128,2048]{2,1,0:T(8,128)(2,1)}) %all-gather.5.cloned.1.call-update) | async-done | bytes 8388624 | tf_op jit(solution)/shard_map/all_gather | solution.py:55
  84.6 4.0 %gather_fusion.4 = bf16[3,128,2048]{2,1,0:T(8,128)(2,1)S(1)} fusion(bf16[16,128,2048]{2,1,0:T(8,128)(2,1)} %all-gather.5.cloned.1.call-done, s32[1024]{0:T(1024)S(1)} %pad_clamp_fusion), kind=kCustom, calls=%fused_computation.3.clone | custom fusion | bytes 3145740 | tf_op jit(solution)/shard_map/jit(_take)/gather | solution.py:62
  88.6 4.0 %gather_fusion.2 = bf16[3,128,2048]{2,1,0:T(8,128)(2,1)S(1)} fusion(bf16[16,128,2048]{2,1,0:T(8,128)(2,1)} %all-gather.5.cloned.1.call-done, s32[1024]{0:T(1024)S(1)} %pad_clamp_fusion.2), kind=kCustom, calls=%fused_computation.1.clone | custom fusion | bytes 3145740 | tf_op jit(solution)/shard_map/jit(_take)/gather | solution.py:62
  94.7 85.7 %all-gather.3.cloned.1.call-done = bf16[32,128,2048]{2,1,0:T(8,128)(2,1)} async-done(((bf16[32,8,2048]{2,1,0:T(8,128)(2,1)}), bf16[32,128,2048]{2,1,0:T(8,128)(2,1)}) %all-gather.3.cloned.1.call-update) | async-done | bytes 16777232 | tf_op jit(solution)/shard_map/all_gather | solution.py:54
  180.4 8.1 %gather_fusion.3 = bf16[5,128,2048]{2,1,0:T(8,128)(2,1)} fusion(bf16[32,128,2048]{2,1,0:T(8,128)(2,1)} %all-gather.3.cloned.1.call-done, s32[1024]{0:T(1024)S(1)} %pad_clamp_fusion.1), kind=kCustom, calls=%fused_computation.2.clone | custom fusion | bytes 5242900 | tf_op jit(solution)/shard_map/jit(_take)/gather | solution.py:61
  188.5 8.1 %gather_fusion.1 = bf16[5,128,2048]{2,1,0:T(8,128)(2,1)} fusion(bf16[32,128,2048]{2,1,0:T(8,128)(2,1)} %all-gather.3.cloned.1.call-done, s32[1024]{0:T(1024)S(1)} %pad_clamp_fusion.4), kind=kCustom, calls=%fused_computation.clone | custom fusion | bytes 5242900 | tf_op jit(solution)/shard_map/jit(_take)/gather | solution.py:61
  196.7 3.2 %broadcast_select_fusion = (bf16[5,128,2048]{2,1,0:T(8,128)(2,1)S(1)}, bf16[5,128,2048]{2,1,0:T(8,128)(2,1)S(1)}) fusion(bf16[5,128,2048]{2,1,0:T(8,128)(2,1)} %gather_fusion.3, pred[5]{0:T(512)(128)(4,1)S(1)} %get-tuple-element.37, bf16[5,128,2048]{2,1,0:T(8,128)(2,1)} %gather_fusion.1, pred[5]{0:T(512)(128)(4,1)S(1)} %get-tuple-element.11), kind=kLoop, calls=%fused_computation.42 | loop fusion | flops 2621440 | bytes 10485770 | tf_op jit(solution)/shard_map/jit(_take)/select_n | solution.py:61
  202.1 3.9 %copy.43 = bf16[8,128,1024]{1,2,0:T(8,128)(2,1)} copy(bf16[8,128,1024]{2,1,0:T(8,128)(2,1)} %get-tuple-element.21) | data formatting | bytes 4194304 | tf_op jit(solution)/shard_map/slice | solution.py:19
  206.0 3.1 %fusion.66 = (bf16[8,128,4,128]{1,3,2,0:T(8,128)(2,1)}, bf16[8,128,4,128]{1,3,2,0:T(8,128)(2,1)}) fusion(bf16[8,128,8,128]{1,3,2,0:T(8,128)(2,1)} %bitcast.206), kind=kLoop, calls=%fused_computation.115 | loop fusion | bytes 4194304 | tf_op jit(solution)/shard_map/slice | solution.py:29
  209.1 3.9 %copy.45 = bf16[8,128,1024]{1,2,0:T(8,128)(2,1)} copy(bf16[8,128,1024]{2,1,0:T(8,128)(2,1)} %get-tuple-element.22) | data formatting | bytes 4194304 | tf_op jit(solution)/shard_map/slice | solution.py:16
  213.0 3.1 %fusion.67 = (bf16[8,128,4,128]{1,3,2,0:T(8,128)(2,1)}, bf16[8,128,4,128]{1,3,2,0:T(8,128)(2,1)}) fusion(bf16[8,128,8,128]{1,3,2,0:T(8,128)(2,1)} %bitcast.207), kind=kLoop, calls=%fused_computation.116 | loop fusion | bytes 4194304 | tf_op jit(solution)/shard_map/slice | solution.py:28
  220.7 3.4 %fusion.25 = (bf16[8,128,1024]{2,1,0:T(8,128)(2,1)}, bf16[8,128,1024]{2,1,0:T(8,128)(2,1)}) fusion(bf16[5,128,2048]{2,1,0:T(8,128)(2,1)S(1)} %get-tuple-element.48, bf16[3,128,2048]{2,1,0:T(8,128)(2,1)} %get-tuple-element.50), kind=kLoop, calls=%fused_computation.45 | loop fusion | flops 8388608 | bytes 8388608 | tf_op jit(solution)/shard_map/concatenate | solution.py:59
  224.2 3.0 copy.32
  228.7 3.0 copy.34
  237.9 6.3 %bitcast_reduce_fusion.1 = (f32[128,4,6]{0,2,1:T(8,128)S(1)}, f32[4,8,128,128,6]{3,2,4,1,0:T(8,128)}) fusion(pred[8]{0:T(512)(128)(4,1)S(1)} %get-tuple-element.52, bf16[128,8,6,128]{0,3,2,1:T(8,128)(2,1)S(1)} %bitcast.214, bf16[8,128,4,128]{3,1,0,2:T(8,128)(2,1)S(1)} %copy-done.1), kind=kOutput, calls=%fused_computation.9 | convolution fusion | flops 814740480 | bytes 14430720 | tf_op jit(solution)/shard_map/qgrd,pkgd->qgrpk/dot_general | solution.py:30
  244.2 7.5 %fusion.8 = (f32[128,4,6]{0,2,1:T(8,128)S(1)}, f32[128,4,6]{0,2,1:T(8,128)S(1)}, f32[4,8,128,128,6]{3,2,4,1,0:T(8,128)S(1)}) fusion(f32[4,8,128,128,6]{3,2,4,1,0:T(8,128)} %get-tuple-element.42, f32[128,4,6]{0,2,1:T(8,128)S(1)} %get-tuple-element.41, pred[8]{0:T(512)(128)(4,1)S(1)} %get-tuple-element.52, bf16[128,8,6,128]{0,3,2,1:T(8,128)(2,1)S(1)} %bitcast.215, ...), kind=kOutput, calls=%fused_computation.25 | convolution fusion | flops 827320320 | bytes 27042304 | tf_op jit(solution)/shard_map/qgrd,pkgd->qgrpk/dot_general | solution.py:30
  251.7 7.6 %fusion.27 = bf16[128,4,6,128]{0,3,2,1:T(8,128)(2,1)S(1)} fusion(f32[4,8,128,128,6]{3,2,4,1,0:T(8,128)} %get-tuple-element.42, f32[128,4,6]{0,2,1:T(8,128)S(1)} %get-tuple-element.41, pred[8]{0:T(512)(128)(4,1)S(1)} %get-tuple-element.52, bf16[8,128,4,128]{1,3,2,0:T(8,128)(2,1)S(1)} %copy-done.9, f32[128,4,6]{0,2,1:T(8,128)S(1)} %get-tuple-element.9), kind=kOutput, calls=%fused_computation.51 | convolution fusion | flops 818675712 | bytes 14442504 | tf_op jit(solution)/shard_map/qgrpk,pkgd->qgrd/dot_general | solution.py:39
  261.9 3.3 %fusion.26 = bf16[128,4,6,128]{0,3,2,1:T(8,128)(2,1)S(1)} fusion(f32[4,8,128,128,6]{3,2,4,1,0:T(8,128)S(1)} %get-tuple-element.43, f32[128,4,6]{0,2,1:T(8,128)S(1)} %get-tuple-element.10, pred[8]{0:T(512)(128)(4,1)S(1)} %get-tuple-element.52, bf16[8,128,4,128]{1,3,2,0:T(8,128)(2,1)S(1)} %copy-done.7, f32[128,4,6]{0,2,1:T(8,128)S(1)} %fusion.10), kind=kOutput, calls=%fused_computation.49 | convolution fusion | flops 818675712 | bytes 14442504 | tf_op jit(solution)/shard_map/qgrpk,pkgd->qgrd/dot_general | solution.py:39
  266.0 7.9 %bitcast_reduce_fusion.3 = (f32[128,4,6]{0,2,1:T(8,128)S(1)}, f32[4,8,128,128,6]{3,2,4,1,0:T(8,128)}) fusion(pred[8]{0:T(512)(128)(4,1)S(1)} %get-tuple-element.51, bf16[128,8,6,128]{0,3,2,1:T(8,128)(2,1)} %bitcast.212, bf16[8,128,4,128]{3,1,0,2:T(8,128)(2,1)} %copy.81), kind=kOutput, calls=%fused_computation.15 | convolution fusion | flops 814740480 | bytes 14430216 | tf_op jit(solution)/shard_map/qgrd,pkgd->qgrpk/dot_general | solution.py:30
  273.9 7.5 %fusion.4 = (f32[128,4,6]{0,2,1:T(8,128)S(1)}, f32[128,4,6]{0,2,1:T(8,128)S(1)}, f32[4,8,128,128,6]{3,2,4,1,0:T(8,128)S(1)}) fusion(f32[4,8,128,128,6]{3,2,4,1,0:T(8,128)} %get-tuple-element.45, f32[128,4,6]{0,2,1:T(8,128)S(1)} %get-tuple-element.44, pred[8]{0:T(512)(128)(4,1)S(1)} %get-tuple-element.51, bf16[128,8,6,128]{0,3,2,1:T(8,128)(2,1)S(1)} %bitcast.213, ...), kind=kOutput, calls=%fused_computation.21 | convolution fusion | flops 827320320 | bytes 27042304 | tf_op jit(solution)/shard_map/qgrd,pkgd->qgrpk/dot_general | solution.py:30
  281.4 7.6 %fusion.29 = bf16[128,4,6,128]{0,3,2,1:T(8,128)(2,1)S(1)} fusion(f32[4,8,128,128,6]{3,2,4,1,0:T(8,128)} %get-tuple-element.45, f32[128,4,6]{0,2,1:T(8,128)S(1)} %get-tuple-element.44, pred[8]{0:T(512)(128)(4,1)S(1)} %get-tuple-element.51, bf16[8,128,4,128]{1,3,2,0:T(8,128)(2,1)S(1)} %copy-done.8, f32[128,4,6]{0,2,1:T(8,128)S(1)} %get-tuple-element.6), kind=kOutput, calls=%fused_computation.55 | convolution fusion | flops 818675712 | bytes 14442504 | tf_op jit(solution)/shard_map/qgrpk,pkgd->qgrd/dot_general | solution.py:39
  291.6 3.3 %fusion.28 = bf16[128,4,6,128]{0,3,2,1:T(8,128)(2,1)S(1)} fusion(f32[4,8,128,128,6]{3,2,4,1,0:T(8,128)S(1)} %get-tuple-element.46, f32[128,4,6]{0,2,1:T(8,128)S(1)} %get-tuple-element.8, pred[8]{0:T(512)(128)(4,1)S(1)} %get-tuple-element.51, bf16[8,128,4,128]{1,3,2,0:T(8,128)(2,1)S(1)} %copy-done.6, f32[128,4,6]{0,2,1:T(8,128)S(1)} %fusion.6), kind=kOutput, calls=%fused_computation.53 | convolution fusion | flops 818675712 | bytes 14442504 | tf_op jit(solution)/shard_map/qgrpk,pkgd->qgrd/dot_general | solution.py:39
  296.6 3.3 %pad_maximum_fusion = bf16[256,6144]{1,0:T(8,128)(2,1)} fusion(bf16[128,6144]{1,0:T(8,128)(2,1)S(1)} %copy.55, bf16[128,6144]{1,0:T(8,128)(2,1)} %copy.54), kind=kLoop, calls=%fused_computation.41 | loop fusion | flops 6291456 | bytes 6291456 | tf_op jit(solution)/shard_map/concatenate | solution.py:69
  (59 shorter events, 33.5 us)
Async XLA Ops:
  6.5 78.1 %all-gather.5.cloned.1.call-start = ((), (), s32[]{:S(2)}) async-start(), calls=%async_computation.2 | async-start | bytes 8912896 | tf_op jit(solution)/shard_map/all_gather | solution.py:55
  27.7 152.7 %all-gather.3.cloned.1.call-start = ((), (), s32[]{:S(2)}) async-start(), calls=%async_computation.1 | async-start | bytes 17825792 | tf_op jit(solution)/shard_map/all_gather | solution.py:54
  30.6 3.2 %copy-start.11 = (s32[2,5]{1,0:T(2,128)S(1)}, s32[2,5]{1,0:T(2,128)}, u32[]{:S(2)}) copy-start(s32[2,5]{1,0:T(2,128)} %param.11) | copy-start | bytes 124
  30.6 3.2 %copy-start.10 = (s32[2,3]{1,0:T(2,128)S(1)}, s32[2,3]{1,0:T(2,128)}, u32[]{:S(2)}) copy-start(s32[2,3]{1,0:T(2,128)} %param.12) | copy-start | bytes 76
  196.7 3.2 %copy-start = (bf16[3,128,2048]{2,1,0:T(8,128)(2,1)S(1)}, bf16[3,128,2048]{2,1,0:T(8,128)(2,1)}, u32[]{:S(2)}) copy-start(bf16[3,128,2048]{2,1,0:T(8,128)(2,1)} %get-tuple-element.49) | copy-start | bytes 4718596
  231.7 6.2 %copy-start.1 = (bf16[8,128,4,128]{3,1,0,2:T(8,128)(2,1)S(1)}, bf16[8,128,4,128]{3,1,0,2:T(8,128)(2,1)}, u32[]{:S(2)}) copy-start(bf16[8,128,4,128]{3,1,0,2:T(8,128)(2,1)} %copy.88) | copy-start | bytes 3145732
  233.2 4.7 %copy-start.3 = (bf16[128,6144]{0,1:T(8,128)(2,1)S(1)}, bf16[128,6144]{0,1:T(8,128)(2,1)}, u32[]{:S(2)}) copy-start(bf16[128,6144]{0,1:T(8,128)(2,1)} %copy.89) | copy-start | bytes 4718596
  237.9 6.3 %copy-start.5 = (bf16[8,128,4,128]{3,1,0,2:T(8,128)(2,1)S(1)}, bf16[8,128,4,128]{3,1,0,2:T(8,128)(2,1)}, u32[]{:S(2)}) copy-start(bf16[8,128,4,128]{3,1,0,2:T(8,128)(2,1)} %copy.92) | copy-start | bytes 3145732
  244.2 7.5 %copy-start.9 = (bf16[8,128,4,128]{1,3,2,0:T(8,128)(2,1)S(1)}, bf16[8,128,4,128]{1,3,2,0:T(8,128)(2,1)}, u32[]{:S(2)}) copy-start(bf16[8,128,4,128]{1,3,2,0:T(8,128)(2,1)} %get-tuple-element.29) | copy-start | bytes 3145732
  259.3 2.5 copy-start.7
  266.0 7.9 %copy-start.2 = (bf16[128,6144]{0,1:T(8,128)(2,1)S(1)}, bf16[128,6144]{0,1:T(8,128)(2,1)}, u32[]{:S(2)}) copy-start(bf16[128,6144]{0,1:T(8,128)(2,1)} %copy.82) | copy-start | bytes 4718596
  266.0 7.9 %copy-start.4 = (bf16[8,128,4,128]{3,1,0,2:T(8,128)(2,1)S(1)}, bf16[8,128,4,128]{3,1,0,2:T(8,128)(2,1)}, u32[]{:S(2)}) copy-start(bf16[8,128,4,128]{3,1,0,2:T(8,128)(2,1)} %copy.85) | copy-start | bytes 3145732
  273.9 7.5 %copy-start.8 = (bf16[8,128,4,128]{1,3,2,0:T(8,128)(2,1)S(1)}, bf16[8,128,4,128]{1,3,2,0:T(8,128)(2,1)}, u32[]{:S(2)}) copy-start(bf16[8,128,4,128]{1,3,2,0:T(8,128)(2,1)} %get-tuple-element.25) | copy-start | bytes 3145732
  289.1 2.5 copy-start.6
Sparse Core Ops, SparseCore 0:
  27.8 56.7 all-gather.4
  86.5 93.9 all-gather.2
where the time goes:
time: 308 us; the launch traced here: 307 us
  waiting for transfers between devices  137 us (44%)
  local copies, waits for them, and re-layouts  66 us (21%)
  matrix products  51 us (17%)
  other arithmetic  21.1 us (7%)
  blocking collectives  17.9 us (6%)
  between operations  13.7 us (4%)
    all_gather x1, waiting for transfers between devices, shards(): group_pool = lax.all_gather(keys_values, 'member', axis=1, tiled=True)  85.7 us
    all_gather x1, waiting for transfers between devices, shards(): cast_pool = lax.all_gather(arrived, 'member', axis=1, tiled=True)  50.6 us
    dot_general x4, matrix products, attend_rows(): jnp.einsum('qgrd,pkgd->qgrpk', query_part, keys_part, preferred_element_t...  29.2 us
    dot_general x4, matrix products, attend_rows(): jnp.einsum('qgrpk,pkgd->qgrd', rounded, values_part, preferred_element_ty...  21.8 us
    all_to_all x1, blocking collectives, shards(): lax.all_to_all(outgoing, 'group', split_axis=0, concat_axis=0, tiled=True)  17.9 us
    gather x2, local copies, waits for them, and re-layouts, shards(): jnp.take(group_pool, jnp.maximum(local_row, 0), axis=0)  16.3 us
    unnamed x30, local copies, waits for them, and re-layouts  12.5 us
    gather x2, local copies, waits for them, and re-layouts, shards(): jnp.take(cast_pool, jnp.maximum(remote_row, 0), axis=0)  8.06 us
  transfers between devices with their start and end apart: 2, of which 2 were waited for; matrix products, arithmetic and copies ran while one was open for 5% of the time, Pallas kernels for 0%

commit v1 on v0

--- a/solution.py
+++ b/solution.py
@@ -51,7 +51,9 @@
     outputs = []
     outgoing = jnp.take(keys_values, targets, axis=0)
     arrived = lax.all_to_all(outgoing, "group", split_axis=0, concat_axis=0, tiled=True)
-    group_pool = lax.all_gather(keys_values, "member", axis=1, tiled=True)
+    group_pool = jnp.concatenate(
+        lax.all_to_all(jnp.stack([keys_values] * lax.axis_size("member")), "member", 0, 0), axis=1
+    )
     cast_pool = lax.all_gather(arrived, "member", axis=1, tiled=True)
     for query_block in range(query_count):
         local_row = local_lists[query_block]

time: 308 us -> 590 us (1.92)
  waiting for transfers between devices: 137 us -> 387 us
  local copies, waits for them, and re-layouts: 66 us -> 88.3 us
  starting transfers between devices: 0.04 us -> 10.6 us
    all_to_all x0 -> x1, waiting for transfers between devices: none -> 179 us  [shards(): lax.all_to_all(jnp.stack([keys_values] * lax.axis_size('member')), 'membe...]
    all_gather x1, waiting for transfers between devices: 50.6 us -> 207 us  [shards(): cast_pool = lax.all_gather(arrived, 'member', axis=1, tiled=True)]
    all_gather x1 -> x0, waiting for transfers between devices: 85.7 us -> none  [shards(): group_pool = lax.all_gather(keys_values, 'member', axis=1, tiled=True)]
    all_to_all x0 -> x1, local copies, waits for them, and re-layouts: none -> 14.1 us  [shards(): lax.all_to_all(jnp.stack([keys_values] * lax.axis_size('member')), 'membe...]
    all_to_all x0 -> x1, starting transfers between devices: none -> 10.5 us  [shards(): lax.all_to_all(jnp.stack([keys_values] * lax.axis_size('member')), 'membe...]
    another operation x0 -> x1, local copies, waits for them, and re-layouts: none -> 6.89 us  [shards(): jnp.stack([keys_values] * lax.axis_size('member'))]
    unnamed x30 -> x28, local copies, waits for them, and re-layouts: 12.5 us -> 12.4 us
  transfers between devices with their start and end apart: 2 -> 2, of which waited for: 2 -> 2; matrix products, arithmetic and copies ran while one was open for 5% -> 3% of each run, Pallas kernels for 0% -> 0%
where the time goes in v1:
time: 590 us; the launch traced here: 588 us
  waiting for transfers between devices  387 us (66%)
  local copies, waits for them, and re-layouts  88.3 us (15%)
  matrix products  48.9 us (8%)
  other arithmetic  22.2 us (4%)
  blocking collectives  17.9 us (3%)
  between operations  13.7 us (2%)
  starting transfers between devices  10.6 us (2%)
    all_gather x1, waiting for transfers between devices, shards(): cast_pool = lax.all_gather(arrived, 'member', axis=1, tiled=True)  207 us
    all_to_all x1, waiting for transfers between devices, shards(): lax.all_to_all(jnp.stack([keys_values] * lax.axis_size('member')), 'membe...  179 us
    dot_general x4, matrix products, attend_rows(): jnp.einsum('qgrd,pkgd->qgrpk', query_part, keys_part, preferred_element_t...  27.2 us
    dot_general x4, matrix products, attend_rows(): jnp.einsum('qgrpk,pkgd->qgrd', rounded, values_part, preferred_element_ty...  21.7 us
    all_to_all x1, blocking collectives, shards(): lax.all_to_all(outgoing, 'group', split_axis=0, concat_axis=0, tiled=True)  17.9 us
    gather x2, local copies, waits for them, and re-layouts, shards(): jnp.take(group_pool, jnp.maximum(local_row, 0), axis=0)  16.3 us
    all_to_all x1, local copies, waits for them, and re-layouts, shards(): lax.all_to_all(jnp.stack([keys_values] * lax.axis_size('member')), 'membe...  14.1 us
    unnamed x28, local copies, waits for them, and re-layouts  12.4 us
  transfers between devices with their start and end apart: 2, of which 2 were waited for; matrix products, arithmetic and copies ran while one was open for 3% of the time, Pallas kernels for 0%

profile of v1, /device:TPU:1, one launch (start us, length us, event | category | flops | bytes accessed | tf_op | source)
XLA Modules:
  0.0 588.4 jit_solution(4845622094830279754)
XLA Ops:
  9.8 17.9 %all_to_all.10 = bf16[16,8,2048]{2,1,0:T(8,128)(2,1)} all-to-all(bf16[16,8,2048]{2,1,0:T(8,128)(2,1)S(1)} %broadcast_select_fusion.4), channel_id=1, replica_groups=mesh['group'=16,'member'=16] {'group'}, dimensions={0} | all-to-all | bytes 1048576 | tf_op jit(solution)/shard_map/all_to_all | solution.py:53
  27.7 6.9 %stack.2 = bf16[16,32,8,2048]{3,2,1,0:T(8,128)(2,1)} broadcast(bf16[32,8,2048]{2,1,0:T(8,128)(2,1)} %param.10), dimensions={1,2,3} | broadcast | bytes 17825792 | tf_op jit(solution)/shard_map/stack | solution.py:55
  34.6 10.5 %all-to-all-start = ((bf16[16,32,8,2048]{3,2,1,0:T(8,128)(2,1)}), bf16[16,32,8,2048]{3,2,1,0:T(8,128)(2,1)}, u32[]{:S(2)}, u32[]{:S(2)}) async-start(bf16[16,32,8,2048]{3,2,1,0:T(8,128)(2,1)} %stack.2), calls=%async_computation | async-start | bytes 33554432 | tf_op jit(solution)/shard_map/all_to_all | solution.py:55
  51.3 206.9 %all-gather.2.cloned.1.call-done = bf16[16,128,2048]{2,1,0:T(8,128)(2,1)} async-done(((bf16[16,8,2048]{2,1,0:T(8,128)(2,1)}), bf16[16,128,2048]{2,1,0:T(8,128)(2,1)}) %all-gather.2.cloned.1.call-update) | async-done | bytes 8388624 | tf_op jit(solution)/shard_map/all_gather | solution.py:57
  258.2 4.0 gather_fusion.2
  262.3 4.0 gather_fusion.4
  268.3 179.3 %all-to-all-done = bf16[16,32,8,2048]{3,2,1,0:T(8,128)(2,1)} async-done(((bf16[16,32,8,2048]{3,2,1,0:T(8,128)(2,1)}), bf16[16,32,8,2048]{3,2,1,0:T(8,128)(2,1)}, u32[]{:S(2)}, u32[]{:S(2)}) %all-to-all-start) | async-done | bytes 16777248 | tf_op jit(solution)/shard_map/all_to_all | solution.py:55
  447.6 14.1 %copy.116 = bf16[16,32,8,2048]{3,2,0,1:T(8,128)(2,1)} copy(bf16[16,32,8,2048]{3,2,1,0:T(8,128)(2,1)} %all-to-all-done) | data formatting | bytes 33554432 | tf_op jit(solution)/shard_map/all_to_all | solution.py:55
  461.7 8.2 %gather_fusion.1 = bf16[5,128,2048]{2,1,0:T(8,128)(2,1)} fusion(bf16[32,128,2048]{2,1,0:T(8,128)(2,1)} %bitcast.211, s32[1024]{0:T(1024)S(1)} %pad_clamp_fusion.4), kind=kCustom, calls=%fused_computation.clone | custom fusion | bytes 5242900 | tf_op jit(solution)/shard_map/jit(_take)/gather | solution.py:63
  469.8 8.1 %gather_fusion.3 = bf16[5,128,2048]{2,1,0:T(8,128)(2,1)} fusion(bf16[32,128,2048]{2,1,0:T(8,128)(2,1)} %bitcast.212, s32[1024]{0:T(1024)S(1)} %pad_clamp_fusion.1), kind=kCustom, calls=%fused_computation.2.clone | custom fusion | bytes 5242900 | tf_op jit(solution)/shard_map/jit(_take)/gather | solution.py:63
  478.0 3.2 broadcast_select_fusion
  483.4 3.9 copy.39
  487.3 3.1 fusion.65
  495.0 3.9 copy.37
  501.8 6.3 %bitcast_reduce_fusion.3 = (f32[128,4,6]{0,2,1:T(8,128)S(1)}, f32[4,8,128,128,6]{3,2,4,1,0:T(8,128)}) fusion(pred[8]{0:T(512)(128)(4,1)S(1)} %get-tuple-element.51, bf16[128,8,6,128]{0,3,2,1:T(8,128)(2,1)S(1)} %bitcast.221, bf16[8,128,4,128]{3,1,0,2:T(8,128)(2,1)S(1)} %copy-done.2), kind=kOutput, calls=%fused_computation.16 | convolution fusion | flops 814740480 | bytes 14430720 | tf_op jit(solution)/shard_map/qgrd,pkgd->qgrpk/dot_general | solution.py:30
  508.2 7.4 %fusion.4 = (f32[128,4,6]{0,2,1:T(8,128)S(1)}, f32[128,4,6]{0,2,1:T(8,128)S(1)}, f32[4,8,128,128,6]{3,2,4,1,0:T(8,128)S(1)}) fusion(f32[4,8,128,128,6]{3,2,4,1,0:T(8,128)} %get-tuple-element.45, f32[128,4,6]{0,2,1:T(8,128)S(1)} %get-tuple-element.44, pred[8]{0:T(512)(128)(4,1)S(1)} %get-tuple-element.51, bf16[128,8,6,128]{0,3,2,1:T(8,128)(2,1)S(1)} %bitcast.222, ...), kind=kOutput, calls=%fused_computation.22 | convolution fusion | flops 827320320 | bytes 27042304 | tf_op jit(solution)/shard_map/qgrd,pkgd->qgrpk/dot_general | solution.py:30
  515.5 7.6 %fusion.29 = bf16[128,4,6,128]{0,3,2,1:T(8,128)(2,1)S(1)} fusion(f32[4,8,128,128,6]{3,2,4,1,0:T(8,128)} %get-tuple-element.45, f32[128,4,6]{0,2,1:T(8,128)S(1)} %get-tuple-element.44, pred[8]{0:T(512)(128)(4,1)S(1)} %get-tuple-element.51, bf16[8,128,4,128]{1,3,2,0:T(8,128)(2,1)S(1)} %get-tuple-element.25, f32[128,4,6]{0,2,1:T(8,128)S(1)} %get-tuple-element.6), kind=kOutput, calls=%fused_computation.56 | convolution fusion | flops 818675712 | bytes 14442504 | tf_op jit(solution)/shard_map/qgrpk,pkgd->qgrd/dot_general | solution.py:39
  525.7 3.3 fusion.28
  532.8 3.4 fusion.24
  549.6 6.3 %bitcast_reduce_fusion.1 = (f32[128,4,6]{0,2,1:T(8,128)S(1)}, f32[4,8,128,128,6]{3,2,4,1,0:T(8,128)}) fusion(pred[8]{0:T(512)(128)(4,1)S(1)} %get-tuple-element.52, bf16[128,8,6,128]{0,3,2,1:T(8,128)(2,1)S(1)} %bitcast.219, bf16[8,128,4,128]{3,1,0,2:T(8,128)(2,1)S(1)} %copy.93), kind=kOutput, calls=%fused_computation.10 | convolution fusion | flops 814740480 | bytes 14430720 | tf_op jit(solution)/shard_map/qgrd,pkgd->qgrpk/dot_general | solution.py:30
  555.9 7.2 %fusion.8 = (f32[128,4,6]{0,2,1:T(8,128)S(1)}, f32[128,4,6]{0,2,1:T(8,128)S(1)}, f32[4,8,128,128,6]{3,2,4,1,0:T(8,128)S(1)}) fusion(f32[4,8,128,128,6]{3,2,4,1,0:T(8,128)} %get-tuple-element.42, f32[128,4,6]{0,2,1:T(8,128)S(1)} %get-tuple-element.41, pred[8]{0:T(512)(128)(4,1)S(1)} %get-tuple-element.52, bf16[128,8,6,128]{0,3,2,1:T(8,128)(2,1)S(1)} %bitcast.220, ...), kind=kOutput, calls=%fused_computation.26 | convolution fusion | flops 827320320 | bytes 27042304 | tf_op jit(solution)/shard_map/qgrd,pkgd->qgrpk/dot_general | solution.py:30
  563.1 7.6 %fusion.27 = bf16[128,4,6,128]{0,3,2,1:T(8,128)(2,1)S(1)} fusion(f32[4,8,128,128,6]{3,2,4,1,0:T(8,128)} %get-tuple-element.42, f32[128,4,6]{0,2,1:T(8,128)S(1)} %get-tuple-element.41, pred[8]{0:T(512)(128)(4,1)S(1)} %get-tuple-element.52, bf16[8,128,4,128]{1,3,2,0:T(8,128)(2,1)S(1)} %get-tuple-element.29, f32[128,4,6]{0,2,1:T(8,128)S(1)} %get-tuple-element.9), kind=kOutput, calls=%fused_computation.52 | convolution fusion | flops 818675712 | bytes 14442504 | tf_op jit(solution)/shard_map/qgrpk,pkgd->qgrd/dot_general | solution.py:39
  573.2 3.3 fusion.26
  578.2 3.4 pad_maximum_fusion
  (58 shorter events, 45.0 us)
Async XLA Ops:
  34.6 413.0 %all-to-all-start = ((bf16[16,32,8,2048]{3,2,1,0:T(8,128)(2,1)}), bf16[16,32,8,2048]{3,2,1,0:T(8,128)(2,1)}, u32[]{:S(2)}, u32[]{:S(2)}) async-start(bf16[16,32,8,2048]{3,2,1,0:T(8,128)(2,1)} %stack.2), calls=%async_computation | async-start | bytes 33554432 | tf_op jit(solution)/shard_map/all_to_all | solution.py:55
  45.1 213.1 %all-gather.2.cloned.1.call-start = ((), (), s32[]{:S(2)}) async-start(), calls=%async_computation.2 | async-start | bytes 8912896 | tf_op jit(solution)/shard_map/all_gather | solution.py:57
  48.0 3.2 copy-start.9
  48.0 3.2 copy-start.10
  477.9 3.2 copy-start.1
  498.9 2.9 copy-start.2
  498.9 2.9 copy-start.4
  501.8 6.3 %copy-start.6 = (bf16[8,128,4,128]{3,1,0,2:T(8,128)(2,1)S(1)}, bf16[8,128,4,128]{3,1,0,2:T(8,128)(2,1)}, u32[]{:S(2)}) copy-start(bf16[8,128,4,128]{3,1,0,2:T(8,128)(2,1)} %copy.90) | copy-start | bytes 3145732
  523.1 2.6 copy-start.8
  547.8 1.8 copy-start.3
  549.6 6.3 %copy-start.5 = (bf16[8,128,4,128]{3,1,0,2:T(8,128)(2,1)S(1)}, bf16[8,128,4,128]{3,1,0,2:T(8,128)(2,1)}, u32[]{:S(2)}) copy-start(bf16[8,128,4,128]{3,1,0,2:T(8,128)(2,1)} %copy.97) | copy-start | bytes 3145732
  570.7 2.5 copy-start.7
  576.5 1.7 copy-start
Sparse Core Ops, SparseCore 0:
  47.8 210.3 all-gather.1
